TPU v7x, 32 devices: a whole 2x2x4 slice. The times are simulated.
32 devices in a mesh: wide: 4 (over z), narrow: 8 (over y, x, core).
Axes of the slice: x: 2, y: 2, z: 4, core: 2. Of those that a mesh axis runs over, the one named last changes fastest.
Arguments:
- samples: bfloat16 [1024, 2, 102144], P(('wide', 'narrow')), may hold values from -6 to 6
- filter_taps: float32 [16, 256], replicated, may hold values from -1.5 to 1.5
- beam_weights: bfloat16 [256, 2, 2, 512, 1024], P(('narrow', 'wide')), may hold values from -0.1875 to 0.1875
- smooth_kernel: float32 [33, 33], replicated, may hold values from -0.1875 to 0.1875
Outputs:
- detection: float32 [256, 48, 1024], P('narrow', None, 'wide')
All inputs are finite; a program needn't handle non-finite values.
Results may differ from a plain program's by a relative error of at most 0.012.
The roundings to bfloat16 on the way count: a program that leaves them out, or rounds other values in their place, can miss the bound.
Values may be sent and summed in bfloat16 or wider, within the bound.
A program may use at most 320 MiB of HBM per device.

v0:
```python
import jax
import jax.numpy as jnp
from jax import lax
from jax.sharding import PartitionSpec as P

INTEG = 8
HALF = 16


def with_halo(block, sides, width):
    for axis, dim in sides:
        count = lax.axis_size(axis)
        forward = [(i, i + 1) for i in range(count - 1)]
        backward = [(target, source) for source, target in forward]
        low = lax.ppermute(
            lax.slice_in_dim(block, block.shape[dim] - width, None, axis=dim), axis, forward
        )
        high = lax.ppermute(lax.slice_in_dim(block, 0, width, axis=dim), axis, backward)
        block = jnp.concatenate([low, block, high], axis=dim)
    return block


def fourier_rows(points, owner_of):
    column = jnp.arange(points, dtype=jnp.int32)
    channel = owner_of(column)
    phase_index = channel[:, None] * column[None, :] % points
    angles = phase_index.astype(jnp.float32) * jnp.float32(2.0 * jnp.pi / points)
    scale = jnp.float32(1.0 / points**0.5)
    cosine = jnp.cos(angles) * scale
    sine_part = jnp.sin(angles) * scale
    real_row = jnp.stack([cosine, sine_part], axis=1)
    imag_row = jnp.stack([-sine_part, cosine], axis=1)
    return jnp.stack([real_row, imag_row], axis=1).reshape(2 * points, 2, points)


def channelize(segment, filter_taps, fourier_table):
    tap_count, points = filter_taps.shape
    inputs_here = segment.shape[0]
    frames = segment.shape[2] // points
    spectra = frames - tap_count + 1
    signal = segment.astype(jnp.float32).reshape(inputs_here, 2, frames, points)
    windowed = filter_taps[0] * signal[:, :, 0:spectra]
    for tap_index in range(1, tap_count):
        windowed = windowed + filter_taps[tap_index] * signal[:, :, tap_index : tap_index + spectra]
    spectrum = jnp.einsum(
        "pb,isb->ips",
        fourier_table[:, 0],
        windowed[:, 0],
        precision=lax.Precision.HIGH,
        preferred_element_type=jnp.float32,
    )
    spectrum = spectrum + jnp.einsum(
        "pb,isb->ips",
        fourier_table[:, 1],
        windowed[:, 1],
        precision=lax.Precision.HIGH,
        preferred_element_type=jnp.float32,
    )
    return spectrum.astype(jnp.bfloat16).reshape(inputs_here, points, 2, spectra)


def corner_turn(voltage):
    inputs_here, points, part_count, spectra = voltage.shape
    wide_count = lax.axis_size("wide")
    narrow_count = lax.axis_size("narrow")
    per_device = points // (wide_count * narrow_count)
    arranged = voltage.reshape(
        inputs_here, wide_count * narrow_count, per_device, part_count, spectra
    )
    turned = lax.all_to_all(arranged, ("wide", "narrow"), split_axis=1, concat_axis=0, tiled=True)
    return turned.reshape(-1, per_device, part_count, spectra)


def beam_power(turned, beam_weights):
    per_device = turned.shape[1]
    spectra = turned.shape[3]
    pol_count = beam_weights.shape[1]
    dishes = beam_weights.shape[3]
    arranged = turned.reshape(pol_count, dishes, per_device, 2, spectra)
    real_in = arranged[:, :, :, 0]
    imag_in = arranged[:, :, :, 1]
    real_rows = jnp.stack([real_in, -imag_in], axis=0)
    imag_rows = jnp.stack([imag_in, real_in], axis=0)
    extended = jnp.stack([real_rows, imag_rows], axis=0)
    extended = jnp.transpose(extended, (4, 2, 0, 5, 1, 3))
    formed = jnp.einsum(
        "jposrd,jprdb->jposb", extended, beam_weights, preferred_element_type=jnp.float32
    )
    energy = jnp.sum(formed * formed, axis=(1, 2))
    binned = energy.reshape(per_device, spectra // INTEG, INTEG, -1).sum(axis=2)
    return (binned / jnp.float32(pol_count * INTEG)).astype(jnp.bfloat16)


def smooth(extended, smooth_kernel):
    extent = smooth_kernel.shape[0]
    half_width = extent // 2
    channels_here = extended.shape[0] - 2 * half_width
    bin_count = extended.shape[1]
    values = extended.astype(jnp.float32)
    centered = values - jnp.mean(values, axis=1, keepdims=True)
    positions = jnp.arange(bin_count, dtype=jnp.int32)
    distance = positions[None, :] - positions[:, None] + half_width
    selector = (distance[None] == jnp.arange(extent, dtype=jnp.int32)[:, None, None]).astype(
        jnp.float32
    )
    toeplitz = jnp.einsum("kd,dtu->ktu", smooth_kernel, selector, precision=lax.Precision.HIGH)
    result = jnp.zeros((channels_here, bin_count, extended.shape[2]), jnp.float32)
    for offset in range(extent):
        result = result + jnp.einsum(
            "tu,cub->ctb",
            toeplitz[offset],
            centered[offset : offset + channels_here],
            precision=lax.Precision.HIGH,
        )
    return result


def body(samples, filter_taps, beam_weights, smooth_kernel):
    tap_count, points = filter_taps.shape
    wide_count = lax.axis_size("wide")
    narrow_count = lax.axis_size("narrow")
    per_device = points // (wide_count * narrow_count)

    def owner_of(column):
        device_slot = column // per_device
        return (
            device_slot % narrow_count * wide_count + device_slot // narrow_count
        ) * per_device + column % per_device

    fourier_table = fourier_rows(points, owner_of)
    frames = samples.shape[2] // points
    spectra = frames - tap_count + 1
    length = spectra // 3
    pieces = []
    for portion in range(3):
        offset = portion * length * points
        segment = samples[:, :, offset : offset + (length + tap_count - 1) * points]
        pieces.append(
            beam_power(corner_turn(channelize(segment, filter_taps, fourier_table)), beam_weights)
        )
    intensity = jnp.concatenate(pieces, axis=1)
    by_beam = lax.all_to_all(intensity, "wide", split_axis=2, concat_axis=0, tiled=True)
    extended = with_halo(by_beam, (("narrow", 0),), HALF)
    return smooth(extended, smooth_kernel)


def solution(mesh):
    placed = (
        P(("wide", "narrow"), None, None),
        P(),
        P(("narrow", "wide"), None, None, None, None),
        P(),
    )
    return jax.shard_map(
        body, mesh=mesh, in_specs=placed, out_specs=P("narrow", None, "wide"), check_vma=False
    )
```

profile of v0, /device:TPU:4, one launch (start us, length us, event | category | flops | bytes accessed | tf_op | source)
XLA Modules:
  0.0 840.4 jit_solution(2042680482137238214)
XLA Ops:
  0.0 20.4 %slice_convert_fusion.2 = (f32[32,2,36608]{2,1,0:T(2,128)}, f32[32,2,36608]{2,1,0:T(2,128)}, f32[32,2,36608]{2,1,0:T(2,128)}) fusion(bf16[32,2,102144]{2,1,0:T(2,128)(2,1)} %param.4), kind=kLoop, calls=%fused_computation.119 | loop fusion | flops 7028736 | bytes 42172416 | tf_op jit(solution)/shard_map/reshape | solution.py:41
  20.4 12.8 %reshape.327 = f32[32,2,143,256]{3,2,1,0:T(8,128)} reshape(f32[32,2,36608]{2,1,0:T(2,128)} %get-tuple-element.5) | data formatting | bytes 18743296 | tf_op jit(solution)/shard_map/reshape | solution.py:41
  33.2 90.6 %fusion.158 = (f32[32,2,128,256]{3,2,1,0:T(8,128)}, f32[32,2,128,256]{3,2,1,0:T(8,128)}, f32[32,2,128,256]{3,2,1,0:T(8,128)}, f32[32,2,128,256]{3,2,1,0:T(8,128)...) fusion(f32[32,2,143,256]{3,2,1,0:T(8,128)} %reshape.327), kind=kLoop, calls=%fused_computation.277 | loop fusion | bytes 268435456 | tf_op jit(solution)/shard_map/slice | solution.py:42
  127.7 46.2 %fusion.51 = f32[32,2,128,256]{3,2,0,1:T(8,128)} fusion(f32[32,2,128,256]{3,2,1,0:T(8,128)} %get-tuple-element.23, f32[32,2,128,256]{3,2,1,0:T(8,128)} %get-tuple-element.9, f32[32,2,128,256]{3,2,1,0:T(8,128)} %get-tuple-element.10, f32[32,2,128,256]{3,2,1,0:T(8,128)} %get-tuple-element.11, f32[32,2,128,256]{3,2,1,0:T(8,128)} %get-tuple-element.12, ...), kind=kLoop, calls=%fused_computation.84 | loop fusion | flops 65011712 | bytes 142622720 | tf_op jit(solution)/shard_map/add | solution.py:44
  185.6 7.9 copy.83
  193.5 6.2 all-to-all-start
  199.6 12.8 %reshape.328 = f32[32,2,143,256]{3,2,1,0:T(8,128)} reshape(f32[32,2,36608]{2,1,0:T(2,128)} %get-tuple-element.7) | data formatting | bytes 18743296 | tf_op jit(solution)/shard_map/reshape | solution.py:41
  212.4 90.7 %fusion.159 = (f32[32,2,128,256]{3,2,1,0:T(8,128)}, f32[32,2,128,256]{3,2,1,0:T(8,128)}, f32[32,2,128,256]{3,2,1,0:T(8,128)}, f32[32,2,128,256]{3,2,1,0:T(8,128)...) fusion(f32[32,2,143,256]{3,2,1,0:T(8,128)} %reshape.328), kind=kLoop, calls=%fused_computation.278 | loop fusion | bytes 268435456 | tf_op jit(solution)/shard_map/slice | solution.py:42
  303.1 46.2 %fusion.36 = f32[32,2,128,256]{3,2,0,1:T(8,128)} fusion(f32[32,2,128,256]{3,2,1,0:T(8,128)} %get-tuple-element.39, f32[32,2,128,256]{3,2,1,0:T(8,128)} %get-tuple-element.25, f32[32,2,128,256]{3,2,1,0:T(8,128)} %get-tuple-element.26, f32[32,2,128,256]{3,2,1,0:T(8,128)} %get-tuple-element.27, f32[32,2,128,256]{3,2,1,0:T(8,128)} %get-tuple-element.28, ...), kind=kLoop, calls=%fused_computation.53 | loop fusion | flops 65011712 | bytes 142622720 | tf_op jit(solution)/shard_map/add | solution.py:44
  360.6 7.9 copy.89
  368.5 12.8 %reshape.329 = f32[32,2,143,256]{3,2,1,0:T(8,128)} reshape(f32[32,2,36608]{2,1,0:T(2,128)} %get-tuple-element.6) | data formatting | bytes 18743296 | tf_op jit(solution)/shard_map/reshape | solution.py:41
  387.1 90.6 %fusion.160 = (f32[32,2,128,256]{3,2,1,0:T(8,128)}, f32[32,2,128,256]{3,2,1,0:T(8,128)}, f32[32,2,128,256]{3,2,1,0:T(8,128)}, f32[32,2,128,256]{3,2,1,0:T(8,128)...) fusion(f32[32,2,143,256]{3,2,1,0:T(8,128)} %reshape.329), kind=kLoop, calls=%fused_computation.279 | loop fusion | bytes 268435456 | tf_op jit(solution)/shard_map/slice | solution.py:42
  477.8 46.2 %fusion.21 = f32[32,2,128,256]{3,2,0,1:T(8,128)} fusion(f32[32,2,128,256]{3,2,1,0:T(8,128)} %get-tuple-element.55, f32[32,2,128,256]{3,2,1,0:T(8,128)} %get-tuple-element.41, f32[32,2,128,256]{3,2,1,0:T(8,128)} %get-tuple-element.42, f32[32,2,128,256]{3,2,1,0:T(8,128)} %get-tuple-element.43, f32[32,2,128,256]{3,2,1,0:T(8,128)} %get-tuple-element.44, ...), kind=kLoop, calls=%fused_computation.22 | loop fusion | flops 65011712 | bytes 142622720 | tf_op jit(solution)/shard_map/add | solution.py:44
  535.3 8.0 copy.95
  543.3 12.3 %copy.84 = bf16[32,32,1,8,2,128]{5,3,4,2,1,0:T(8,128)(2,1)} copy(bf16[32,32,1,8,2,128]{5,1,4,3,0,2:T(8,128)(2,1)} %bitcast.26) | data formatting | bytes 8388608 | tf_op jit(solution)/shard_map/all_to_all | solution.py:70
  555.6 6.3 all-to-all-start.2
  572.7 10.3 %copy.90 = bf16[32,32,1,8,2,128]{5,3,4,2,1,0:T(8,128)(2,1)S(1)} copy(bf16[32,32,1,8,2,128]{5,1,4,3,0,2:T(8,128)(2,1)} %bitcast.44) | data formatting | bytes 8388608 | tf_op jit(solution)/shard_map/all_to_all | solution.py:70
  599.6 23.3 %fusion.8 = f32[8,128,1024]{2,1,0:T(8,128)} fusion(bf16[8,2,2,512,1024]{4,3,2,1,0:T(8,128)(2,1)} %param.6, bf16[1,2,2,512,8,128]{3,5,1,0,2,4:T(8,128)(2,1)} %get-tuple-element.63, bf16[1,2,2,512,8,128]{3,5,1,0,2,4:T(8,128)(2,1)} %get-tuple-element.62), kind=kOutput, calls=%fused_computation.11 | convolution fusion | flops 8601468928 | bytes 46137344 | tf_op jit(solution)/shard_map/jposrd,jprdb->jposb/dot_general | solution.py:86
  631.3 23.0 %fusion.7 = f32[8,128,1024]{2,1,0:T(8,128)} fusion(bf16[8,2,2,512,1024]{4,3,2,1,0:T(8,128)(2,1)} %param.6, bf16[1,2,2,512,8,128]{3,5,1,0,2,4:T(8,128)(2,1)} %get-tuple-element.65, bf16[1,2,2,512,8,128]{3,5,1,0,2,4:T(8,128)(2,1)} %get-tuple-element.64), kind=kOutput, calls=%fused_computation.9 | convolution fusion | flops 8601468928 | bytes 46137344 | tf_op jit(solution)/shard_map/jposrd,jprdb->jposb/dot_general | solution.py:86
  657.7 10.3 %copy.96 = bf16[32,32,1,8,2,128]{5,3,4,2,1,0:T(8,128)(2,1)S(1)} copy(bf16[32,32,1,8,2,128]{5,1,4,3,0,2:T(8,128)(2,1)} %bitcast.61) | data formatting | bytes 8388608 | tf_op jit(solution)/shard_map/all_to_all | solution.py:70
  679.5 6.3 maximum_bitcast_fusion.10
  685.8 23.1 %fusion.6 = f32[8,128,1024]{2,1,0:T(8,128)} fusion(bf16[8,2,2,512,1024]{4,3,2,1,0:T(8,128)(2,1)} %param.6, bf16[1,2,2,512,8,128]{3,5,1,0,2,4:T(8,128)(2,1)} %get-tuple-element.67, bf16[1,2,2,512,8,128]{3,5,1,0,2,4:T(8,128)(2,1)} %get-tuple-element.66), kind=kOutput, calls=%fused_computation.7 | convolution fusion | flops 8601468928 | bytes 46137344 | tf_op jit(solution)/shard_map/jposrd,jprdb->jposb/dot_general | solution.py:86
  724.1 19.0 %all-to-all-done.3 = bf16[4,2,49152]{2,1,0:T(2,128)(2,1)S(1)} async-done(((bf16[4,2,49152]{2,1,0:T(2,128)(2,1)}), bf16[4,2,49152]{2,1,0:T(2,128)(2,1)S(1)}, u32[]{:S(2)}, u32[]{:S(2)}) %all-to-all-start.3) | async-done | bytes 786464 | tf_op jit(solution)/shard_map/all_to_all | solution.py:142
  822.3 17.9 %bitcast_add_fusion = f32[32,48,256]{2,1,0:T(8,128)} fusion(f32[32,256,48]{1,2,0:T(8,128)} %fusion.76, f32[32,256,48]{1,2,0:T(8,128)} %fusion.77, f32[32,256,48]{1,2,0:T(8,128)} %fusion.78, f32[32,256,48]{1,2,0:T(8,128)} %fusion.79, f32[32,256,48]{1,2,0:T(8,128)} %fusion.80, f32[32,256,48]{1,2,0:T(8,128)} %fusion.81, f32[32,256,48]{1,2,0:T(8,128)} %fusion.82, ...), kind=kOutput, calls=%fused_computation.180 | convolution fusion | flops 131334144 | bytes 53552128 | tf_op jit(solution)/shard_map/tu,cub->ctb/dot_general | solution.py:109
  (107 shorter events, 188.7 us)
Async XLA Ops:
  0.0 722.7 %copy-start = (f32[33,33]{1,0:T(8,128)S(1)}, f32[33,33]{1,0:T(8,128)}, u32[]{:S(2)}) copy-start(f32[33,33]{1,0:T(8,128)} %param.7) | copy-start | bytes 13072
  33.2 90.7 %copy-start.8 = (f32[16,256]{1,0:T(8,128)S(1)}, f32[16,256]{1,0:T(8,128)}, u32[]{:S(2)}) copy-start(f32[16,256]{1,0:T(8,128)} %param.5) | copy-start | bytes 49156
  173.9 5.6 copy-start.2
  193.5 187.8 %all-to-all-start = ((bf16[32,32,8,2,128]{4,0,3,2,1:T(8,128)(2,1)}), bf16[32,32,8,2,128]{4,0,3,2,1:T(8,128)(2,1)}, u32[]{:S(2)}, u32[]{:S(2)}) async-start(bf16[32,32,8,2,128]{4,0,3,2,1:T(8,128)(2,1)} %bitcast.365), calls=%async_computation | async-start | bytes 8388608 | tf_op jit(solution)/shard_map/all_to_all | solution.py:70
  349.3 5.6 copy-start.3
  381.2 174.4 %all-to-all-start.1 = ((bf16[32,32,8,2,128]{4,0,3,2,1:T(8,128)(2,1)}), bf16[32,32,8,2,128]{4,0,3,2,1:T(8,128)(2,1)}, u32[]{:S(2)}, u32[]{:S(2)}) async-start(bf16[32,32,8,2,128]{4,0,3,2,1:T(8,128)(2,1)} %bitcast.363), calls=%async_computation.1 | async-start | bytes 8388608 | tf_op jit(solution)/shard_map/all_to_all | solution.py:70
  524.0 5.6 copy-start.1
  555.6 102.0 %all-to-all-start.2 = ((bf16[32,32,8,2,128]{4,0,3,2,1:T(8,128)(2,1)}), bf16[32,32,8,2,128]{4,0,3,2,1:T(8,128)(2,1)}, u32[]{:S(2)}, u32[]{:S(2)}) async-start(bf16[32,32,8,2,128]{4,0,3,2,1:T(8,128)(2,1)} %bitcast.364), calls=%async_computation.2 | async-start | bytes 8388608 | tf_op jit(solution)/shard_map/all_to_all | solution.py:70
  593.2 2.2 copy-start.4
  593.2 2.9 copy-start.6
  626.1 1.6 copy-start.5
  718.1 25.0 %all-to-all-start.3 = ((bf16[4,2,49152]{2,1,0:T(2,128)(2,1)}), bf16[4,2,49152]{2,1,0:T(2,128)(2,1)S(1)}, u32[]{:S(2)}, u32[]{:S(2)}) async-start(bf16[4,2,49152]{2,1,0:T(2,128)(2,1)} %reshape.333), calls=%async_computation.3 | async-start | bytes 1572864 | tf_op jit(solution)/shard_map/all_to_all | solution.py:142
  746.9 7.6 copy-start.7
  747.6 11.4 %collective-permute-start = (bf16[16,48,256]{2,1,0:T(8,128)(2,1)S(1)}, bf16[16,48,256]{2,1,0:T(8,128)(2,1)S(1)}, u32[]{:S(2)}, u32[]{:S(2)}) collective-permute-start(bf16[16,48,256]{2,1,0:T(8,128)(2,1)S(1)} %bitcast.376), channel_id=1, source_target_pairs={{0,1},{1,2},{2,3},{3,4},{4,5},{5,6},{6,7},{8,9},{9,10},{10,11},{11... | collective-permute-start | bytes 1179656 | tf_op jit(solution)/shard_map/ppermute | solution.py:15
  749.5 10.3 %collective-permute-start.1 = (bf16[16,48,256]{2,1,0:T(8,128)(2,1)S(1)}, bf16[16,48,256]{2,1,0:T(8,128)(2,1)S(1)}, u32[]{:S(2)}, u32[]{:S(2)}) collective-permute-start(bf16[16,48,256]{2,1,0:T(8,128)(2,1)S(1)} %bitcast.377), channel_id=1, source_target_pairs={{1,0},{2,1},{3,2},{4,3},{5,4},{6,5},{7,6},{9,8},{10,9},{11,10},{12... | collective-permute-start | bytes 1179656 | tf_op jit(solution)/shard_map/ppermute | solution.py:18
where the time goes:
time: 854 us; the launch traced here: 840 us
  local copies, waits for them, and re-layouts  413 us (48%)
  other arithmetic  189 us (22%)
  matrix products  185 us (22%)
  starting transfers between devices  29.8 us (3%)
  waiting for transfers between devices  23.7 us (3%)
    slice x4, local copies, waits for them, and re-layouts, channelize(): windowed = filter_taps[0] * signal[:, :, 0:spectra]  272 us
    add x3, other arithmetic, channelize(): windowed + filter_taps[tap_index] * signal[:, :, tap_index:tap_index + sp...  139 us
    dot_general x33, matrix products, smooth(): jnp.einsum('tu,cub->ctb', toeplitz[offset], centered[offset:offset + chan...  79.9 us
    dot_general x3, matrix products, beam_power(): jnp.einsum('jposrd,jprdb->jposb', extended, beam_weights, preferred_eleme...  69.4 us
    reshape x3, local copies, waits for them, and re-layouts, channelize(): signal = segment.astype(jnp.float32).reshape(inputs_here, 2, frames, points)  38.3 us
    all_to_all x3, local copies, waits for them, and re-layouts, corner_turn(): lax.all_to_all(arranged, ('wide', 'narrow'), split_axis=1, concat_axis=0,...  32.9 us
    unnamed x26, local copies, waits for them, and re-layouts  30.2 us
    convert_element_type x3, local copies, waits for them, and re-layouts, channelize(): spectrum.astype(jnp.bfloat16).reshape(inputs_here, points, 2, spectra)  23.8 us
  transfers between devices with their start and end apart: 6, of which 3 were waited for; matrix products, arithmetic and copies ran while one was open for 53% of the time, Pallas kernels for 0%

commit v1 on v0

v1 whole, which is shorter than its diff:
```python
import functools

import jax
import jax.numpy as jnp
from jax import lax
from jax.experimental import pallas as pl
from jax.experimental.pallas import tpu as pltpu
from jax.sharding import PartitionSpec as P

INTEG = 8
HALF = 16
LANES = 128
PORTION = 128
BAND = 8


def with_halo(block, sides, width):
    for axis, dim in sides:
        count = lax.axis_size(axis)
        forward = [(i, i + 1) for i in range(count - 1)]
        backward = [(target, source) for source, target in forward]
        low = lax.ppermute(
            lax.slice_in_dim(block, block.shape[dim] - width, None, axis=dim), axis, forward
        )
        high = lax.ppermute(lax.slice_in_dim(block, 0, width, axis=dim), axis, backward)
        block = jnp.concatenate([low, block, high], axis=dim)
    return block


def fourier_rows(points, owner_of):
    column = jnp.arange(points, dtype=jnp.int32)
    channel = owner_of(column)
    phase_index = channel[:, None] * column[None, :] % points
    angles = phase_index.astype(jnp.float32) * jnp.float32(2.0 * jnp.pi / points)
    scale = jnp.float32(1.0 / points**0.5)
    cosine = jnp.cos(angles) * scale
    sine_part = jnp.sin(angles) * scale
    real_row = jnp.stack([cosine, sine_part], axis=1)
    imag_row = jnp.stack([-sine_part, cosine], axis=1)
    return jnp.stack([real_row, imag_row], axis=1).reshape(2 * points, 2 * points)


def split(value):
    high = value.astype(jnp.bfloat16)
    return high, (value - high.astype(jnp.float32)).astype(jnp.bfloat16)


def channelize_kernel(
    taps_ref, table_ref, main_ref, halo_ref, out_ref, window_ref, high_ref, low_ref, turned_ref
):
    tap_count, points = taps_ref.shape
    group = main_ref.shape[1]
    spectra = main_ref.shape[2] // points
    high_ref[...], low_ref[...] = split(table_ref[...])
    blocks = spectra // tap_count

    for part in range(2):
        for tile in range(points // LANES):
            lane = tile * LANES
            column = part * (points // LANES) + tile
            for base in range(0, group, 8):
                coeffs = [
                    jnp.broadcast_to(taps_ref[tap : tap + 1, lane : lane + LANES], (8, LANES))
                    for tap in range(tap_count)
                ]

                def load(ref, frame):
                    start = pl.multiple_of(frame * points + lane, LANES)
                    rows = ref[part, base : base + 8, pl.ds(start, LANES)]
                    return rows.astype(jnp.float32)

                def emit(block, older, newer_ref, newer_base):
                    sums = list(older)
                    nexts = [None] * tap_count
                    for step in range(tap_count):
                        value = load(newer_ref, newer_base + step)
                        for index in range(tap_count):
                            tap = tap_count + step - index
                            if tap < tap_count:
                                sums[index] = sums[index] + coeffs[tap] * value
                            tap = step - index
                            if 0 <= tap:
                                term = coeffs[tap] * value
                                nexts[index] = (
                                    term if nexts[index] is None else nexts[index] + term
                                )
                        window_ref[
                            column,
                            pl.ds(base * spectra + block * tap_count + step, 8, stride=spectra),
                            :,
                        ] = sums[step]
                    return tuple(nexts)

                first = [None] * tap_count
                for step in range(tap_count):
                    value = load(main_ref, step)
                    for index in range(step + 1):
                        term = coeffs[step - index] * value
                        first[index] = term if first[index] is None else first[index] + term

                def body(block, older):
                    return emit(block, older, main_ref, (block + 1) * tap_count)

                older = lax.fori_loop(0, blocks - 1, body, tuple(first))
                sums = list(older)
                window_ref[
                    column,
                    pl.ds(base * spectra + (blocks - 1) * tap_count, 8, stride=spectra),
                    :,
                ] = sums[0]
                for step in range(tap_count - 1):
                    value = load(halo_ref, step)
                    for index in range(step + 1, tap_count):
                        sums[index] = sums[index] + coeffs[tap_count + step - index] * value
                    window_ref[
                        column,
                        pl.ds(
                            base * spectra + (blocks - 1) * tap_count + step + 1, 8, stride=spectra
                        ),
                        :,
                    ] = sums[step + 1]

    columns = window_ref.shape[0]
    contract = (((1,), (1,)), ((), ()))

    @pl.loop(0, group)
    def _(index):
        rows = pl.ds(pl.multiple_of(index * spectra, spectra), spectra)
        signal = jnp.concatenate([window_ref[column, rows, :] for column in range(columns)], axis=1)
        high, low = split(signal)
        product = functools.partial(
            lax.dot_general, dimension_numbers=contract, preferred_element_type=jnp.float32
        )
        result = (
            product(low_ref[...], high) + product(high_ref[...], low) + product(high_ref[...], high)
        )
        turned_ref[pl.ds(index, result.shape[0], stride=group), :] = result

    out_ref[...] = turned_ref[...].reshape(out_ref.shape).astype(out_ref.dtype)


def channelize(by_part, filter_taps, table, portion):
    tap_count, points = filter_taps.shape
    inputs_here = by_part.shape[1]
    group = min(16, inputs_here)
    rows = table.shape[0]
    halo = tap_count * points
    return pl.pallas_call(
        channelize_kernel,
        grid=(inputs_here // group,),
        in_specs=[
            pl.BlockSpec(filter_taps.shape, lambda g: (0, 0)),
            pl.BlockSpec(table.shape, lambda g: (0, 0)),
            pl.BlockSpec((2, group, PORTION * points), lambda g: (0, g, portion)),
            pl.BlockSpec(
                (2, group, halo), lambda g: (0, g, (portion + 1) * (PORTION // tap_count))
            ),
        ],
        out_specs=pl.BlockSpec((rows, group, PORTION), lambda g: (0, g, 0)),
        out_shape=jax.ShapeDtypeStruct((rows, inputs_here, PORTION), jnp.bfloat16),
        scratch_shapes=[
            pltpu.VMEM((2 * points // LANES, group * PORTION, LANES), jnp.float32),
            pltpu.VMEM(table.shape, jnp.bfloat16),
            pltpu.VMEM(table.shape, jnp.bfloat16),
            pltpu.VMEM((rows * group, PORTION), jnp.float32),
        ],
        cost_estimate=pl.CostEstimate(
            flops=6 * rows * rows * inputs_here * PORTION,
            bytes_accessed=8 * inputs_here * points * PORTION,
            transcendentals=0,
        ),
        compiler_params=pltpu.CompilerParams(vmem_limit_bytes=48 * 1024 * 1024),
        name=f"channelize_{portion}",
    )(filter_taps, table, by_part, by_part)


def beam_kernel(voltage_ref, weight_ref, out_ref):
    sources, _, inputs_each, spectra = voltage_ref.shape
    pols, _, dishes, beams = weight_ref.shape[1:]
    per_pol = sources // pols

    def dish_rows(pol, part):
        rows = voltage_ref[pol * per_pol : (pol + 1) * per_pol, part]
        if inputs_each % 16 != 0:
            rows = rows.astype(jnp.float32)
        return rows.reshape(dishes, spectra).astype(jnp.float32).T.astype(jnp.bfloat16)

    energy = None
    for pol in range(pols):
        real = dish_rows(pol, 0)
        imag = dish_rows(pol, 1)
        left = jnp.concatenate(
            [jnp.concatenate([real, -imag], axis=1), jnp.concatenate([imag, real], axis=1)], axis=0
        )
        weights = weight_ref[0, pol].reshape(2 * dishes, beams)
        formed = jnp.dot(left, weights, preferred_element_type=jnp.float32)
        squares = formed * formed
        power = squares[:spectra] + squares[spectra:]
        energy = power if energy is None else energy + power
    binned = energy.reshape(spectra // INTEG, INTEG, beams).sum(axis=1)
    out_ref[0] = (binned * jnp.float32(1.0 / (pols * INTEG))).astype(jnp.bfloat16)


def beam_power(turned, beam_weights, portion):
    sources, rows, inputs_each, spectra = turned.shape
    per_device, pols, _, dishes, beams = beam_weights.shape
    return pl.pallas_call(
        beam_kernel,
        grid=(per_device,),
        in_specs=[
            pl.BlockSpec((sources, 2, inputs_each, spectra), lambda c: (0, c, 0, 0)),
            pl.BlockSpec((1, pols, 2, dishes, beams), lambda c: (c, 0, 0, 0, 0)),
        ],
        out_specs=pl.BlockSpec((1, spectra // INTEG, beams), lambda c: (c, 0, 0)),
        out_shape=jax.ShapeDtypeStruct((per_device, spectra // INTEG, beams), jnp.bfloat16),
        cost_estimate=pl.CostEstimate(
            flops=16 * per_device * dishes * spectra * beams,
            bytes_accessed=2 * beam_weights.size + 2 * turned.size,
            transcendentals=0,
        ),
        compiler_params=pltpu.CompilerParams(vmem_limit_bytes=48 * 1024 * 1024),
        name=f"beams_{portion}",
    )(turned, beam_weights)


def band_matrix(smooth_kernel, bin_count):
    extent = smooth_kernel.shape[0]
    half_width = extent // 2
    span = BAND + extent - 1
    offsets = jnp.arange(extent, dtype=jnp.int32)
    bins = jnp.arange(bin_count, dtype=jnp.int32)
    distance = bins[None, :] - bins[:, None] + half_width
    in_time = (distance[None] == offsets[:, None, None]).astype(jnp.float32)
    steps = jnp.arange(span, dtype=jnp.int32)[None, :] - jnp.arange(BAND, dtype=jnp.int32)[:, None]
    in_band = (steps[None] == offsets[:, None, None]).astype(jnp.float32)
    rows = jnp.einsum("kcj,kd->cjd", in_band, smooth_kernel, precision=lax.Precision.HIGHEST)
    matrix = jnp.einsum("cjd,dtu->ctju", rows, in_time, precision=lax.Precision.HIGHEST)
    return matrix.reshape(BAND * bin_count, span * bin_count)


def smooth(extended, matrix, half_width):
    channels_here = extended.shape[0] - 2 * half_width
    bin_count, beams = extended.shape[1:]
    values = extended.astype(jnp.float32)
    centered = values - jnp.mean(values, axis=1, keepdims=True)
    flat = centered.reshape(-1, beams)
    pieces = []
    for start in range(0, channels_here, BAND):
        rows = lax.slice_in_dim(flat, start * bin_count, start * bin_count + matrix.shape[1], axis=0)
        pieces.append(
            jnp.dot(
                matrix, rows, precision=lax.Precision.HIGH, preferred_element_type=jnp.float32
            )
        )
    return jnp.concatenate(pieces, axis=0).reshape(channels_here, bin_count, beams)


def body(samples, filter_taps, beam_weights, smooth_kernel):
    tap_count, points = filter_taps.shape
    wide_count = lax.axis_size("wide")
    narrow_count = lax.axis_size("narrow")
    devices = wide_count * narrow_count
    per_device = points // devices

    def owner_of(column):
        device_slot = column // per_device
        return (
            device_slot % narrow_count * wide_count + device_slot // narrow_count
        ) * per_device + column % per_device

    table = fourier_rows(points, owner_of)
    frames = samples.shape[2] // points
    spectra = frames - tap_count + 1
    by_part = jnp.transpose(samples, (1, 0, 2))
    matrix = band_matrix(smooth_kernel, spectra // INTEG)
    turned = []
    for portion in range(spectra // PORTION):
        voltage = channelize(by_part, filter_taps, table, portion)
        arranged = voltage.reshape(devices, 2 * per_device, -1, PORTION)
        turned.append(
            lax.all_to_all(arranged, ("wide", "narrow"), split_axis=0, concat_axis=0, tiled=True)
        )
    pieces = [beam_power(block, beam_weights, portion) for portion, block in enumerate(turned)]
    intensity = jnp.concatenate(pieces, axis=1)
    by_beam = lax.all_to_all(intensity, "wide", split_axis=2, concat_axis=0, tiled=True)
    half_width = smooth_kernel.shape[0] // 2
    extended = with_halo(by_beam, (("narrow", 0),), half_width)
    return smooth(extended, matrix, half_width)


def solution(mesh):
    placed = (
        P(("wide", "narrow"), None, None),
        P(),
        P(("narrow", "wide"), None, None, None, None),
        P(),
    )
    return jax.shard_map(
        body, mesh=mesh, in_specs=placed, out_specs=P("narrow", None, "wide"), check_vma=False
    )
```

time: 854 us -> 431 us (0.50); the launches traced: 840 us -> 430 us
  local copies, waits for them, and re-layouts: 413 us -> 41.9 us
  other arithmetic: 189 us -> 5.31 us
  matrix products: 185 us -> 9.6 us
  waiting for transfers between devices: 23.7 us -> 193 us
  Pallas kernels: 0 us -> 155 us
    slice x9 -> x1, local copies, waits for them, and re-layouts: 282 us -> 1 us  [smooth(): lax.slice_in_dim(flat, start * bin_count, start * bin_count + matrix.shap...]
    dot_general x43 -> x6, matrix products: 185 us -> 9.6 us  [the longest x4 6.06 us: smooth(): jnp.dot(matrix, rows, precision=lax.Precision.HIGH, preferred_element_typ...]
    all_to_all x3, waiting for transfers between devices: 0.01 us -> 173 us  [body(): lax.all_to_all(arranged, ('wide', 'narrow'), split_axis=0, concat_axis=0,...]
    pallas_call x0 -> x6, Pallas kernels: none -> 155 us  [the longest x3 102 us: channelize(): pl.pallas_call(channelize_kernel, grid=(inputs_here // group,), in_specs=...]
    add x4 -> x1, other arithmetic: 139 us -> 0.01 us  [band_matrix(): distance = bins[None, :] - bins[:, None] + half_width]
    reshape x4 -> x1, local copies, waits for them, and re-layouts: 39 us -> 5.66 us  [band_matrix(): return matrix.reshape(BAND * bin_count, span * bin_count)]
    all_to_all x3 -> x0, local copies, waits for them, and re-layouts: 32.9 us -> none  [corner_turn(): lax.all_to_all(arranged, ('wide', 'narrow'), split_axis=1, concat_axis=0,...]
    convert_element_type x3 -> x0, local copies, waits for them, and re-layouts: 23.8 us -> none  [channelize(): spectrum.astype(jnp.bfloat16).reshape(inputs_here, points, 2, spectra)]
  transfers between devices with their start and end apart: 6 -> 6, of which waited for: 3 -> 4; matrix products, arithmetic and copies ran while one was open for 53% -> 3% of each run, Pallas kernels for 0% -> 24%
where the time goes in v1:
time: 431 us; the launch traced here: 430 us
  waiting for transfers between devices  193 us (45%)
  Pallas kernels  155 us (36%)
  local copies, waits for them, and re-layouts  41.9 us (10%)
  starting transfers between devices  25.4 us (6%)
  matrix products  9.6 us (2%)
  other arithmetic  5.31 us (1%)
    all_to_all x3, waiting for transfers between devices, body(): lax.all_to_all(arranged, ('wide', 'narrow'), split_axis=0, concat_axis=0,...  173 us
    pallas_call x3, Pallas kernels, channelize(): pl.pallas_call(channelize_kernel, grid=(inputs_here // group,), in_specs=...  102 us
    pallas_call x3, Pallas kernels, beam_power(): pl.pallas_call(beam_kernel, grid=(per_device,), in_specs=[pl.BlockSpec((s...  52.4 us
    unnamed x16, local copies, waits for them, and re-layouts  23.9 us
    all_to_all x1, waiting for transfers between devices, body(): lax.all_to_all(intensity, 'wide', split_axis=2, concat_axis=0, tiled=True)  19.7 us
    all_to_all x3, starting transfers between devices, body(): lax.all_to_all(arranged, ('wide', 'narrow'), split_axis=0, concat_axis=0,...  15.2 us
  transfers between devices with their start and end apart: 6, of which 4 were waited for; matrix products, arithmetic and copies ran while one was open for 3% of the time, Pallas kernels for 24%

profile of v1, /device:TPU:4, one launch (start us, length us, event | category | flops | bytes accessed | tf_op | source)
XLA Modules:
  0.0 430.1 jit_solution(3035675224886991955)
XLA Ops:
  2.2 11.8 %copy.35 = bf16[32,2,102144]{2,0,1:T(8,128)(2,1)} copy(bf16[32,2,102144]{2,1,0:T(2,128)(2,1)} %param.4) | data formatting | bytes 26148864 | tf_op args[0]
  14.0 34.1 %channelize_0.1 = bf16[512,32,128]{2,1,0:T(8,128)(2,1)S(1)} custom-call(f32[16,256]{1,0:T(8,128)S(1)} %copy-done.4, f32[512,512]{1,0:T(8,128)S(1)} %bitcast.48, bf16[2,32,102144]{2,1,0:T(8,128)(2,1)} %bitcast.54, bf16[2,32,102144]{2,1,0:T(8,128)(2,1)} %bitcast.55), custom_call_target="tpu_custom_call" | custom-call | flops 6442450944 | bytes 8388608 | tf_op jit(solution)/shard_map/channelize_0/pallas_call | solution.py:148
  48.1 2.0 copy-done.3
  50.1 6.2 %all-to-all-start = ((bf16[32,16,32,128]{3,2,1,0:T(8,128)(2,1)}), bf16[32,16,32,128]{3,2,1,0:T(8,128)(2,1)}, u32[]{:S(2)}, u32[]{:S(2)}) async-start(bf16[32,16,32,128]{3,2,1,0:T(8,128)(2,1)} %bitcast.53), calls=%async_computation | async-start | bytes 8388608 | tf_op jit(solution)/shard_map/all_to_all | solution.py:281
  56.2 34.1 %channelize_1.1 = bf16[512,32,128]{2,1,0:T(8,128)(2,1)S(1)} custom-call(f32[16,256]{1,0:T(8,128)S(1)} %copy-done.4, f32[512,512]{1,0:T(8,128)S(1)} %bitcast.49, bf16[2,32,102144]{2,1,0:T(8,128)(2,1)} %bitcast.56, bf16[2,32,102144]{2,1,0:T(8,128)(2,1)} %bitcast.57), custom_call_target="tpu_custom_call" | custom-call | flops 6442450944 | bytes 8388608 | tf_op jit(solution)/shard_map/channelize_1/pallas_call | solution.py:148
  90.4 2.0 copy-done.2
  92.4 57.3 %all-to-all-done.voltage_ref = bf16[32,16,32,128]{3,2,1,0:T(8,128)(2,1)} async-done(((bf16[32,16,32,128]{3,2,1,0:T(8,128)(2,1)}), bf16[32,16,32,128]{3,2,1,0:T(8,128)(2,1)}, u32[]{:S(2)}, u32[]{:S(2)}) %all-to-all-start) | async-done | bytes 4194336 | tf_op jit(solution)/shard_map/all_to_all | solution.py:281
  149.6 4.5 %all-to-all-start.1 = ((bf16[32,16,32,128]{3,2,1,0:T(8,128)(2,1)}), bf16[32,16,32,128]{3,2,1,0:T(8,128)(2,1)}, u32[]{:S(2)}, u32[]{:S(2)}) async-start(bf16[32,16,32,128]{3,2,1,0:T(8,128)(2,1)} %bitcast.52), calls=%async_computation.1 | async-start | bytes 8388608 | tf_op jit(solution)/shard_map/all_to_all | solution.py:281
  154.2 34.1 %channelize_2.1 = bf16[512,32,128]{2,1,0:T(8,128)(2,1)S(1)} custom-call(f32[16,256]{1,0:T(8,128)S(1)} %copy-done.4, f32[512,512]{1,0:T(8,128)S(1)} %bitcast.50, bf16[2,32,102144]{2,1,0:T(8,128)(2,1)} %bitcast.58, bf16[2,32,102144]{2,1,0:T(8,128)(2,1)} %bitcast.59), custom_call_target="tpu_custom_call" | custom-call | flops 6442450944 | bytes 8388608 | tf_op jit(solution)/shard_map/channelize_2/pallas_call | solution.py:148
  188.3 2.0 copy-done.1
  190.3 57.3 %all-to-all-done.1.voltage_ref = bf16[32,16,32,128]{3,2,1,0:T(8,128)(2,1)} async-done(((bf16[32,16,32,128]{3,2,1,0:T(8,128)(2,1)}), bf16[32,16,32,128]{3,2,1,0:T(8,128)(2,1)}, u32[]{:S(2)}, u32[]{:S(2)}) %all-to-all-start.1) | async-done | bytes 4194336 | tf_op jit(solution)/shard_map/all_to_all | solution.py:281
  247.6 4.5 %all-to-all-start.2 = ((bf16[32,16,32,128]{3,2,1,0:T(8,128)(2,1)}), bf16[32,16,32,128]{3,2,1,0:T(8,128)(2,1)}, u32[]{:S(2)}, u32[]{:S(2)}) async-start(bf16[32,16,32,128]{3,2,1,0:T(8,128)(2,1)} %bitcast.51), calls=%async_computation.2 | async-start | bytes 8388608 | tf_op jit(solution)/shard_map/all_to_all | solution.py:281
  252.1 17.5 %beams_0.1 = bf16[8,16,1024]{2,1,0:T(8,128)(2,1)S(1)} custom-call(bf16[32,16,32,128]{3,2,1,0:T(8,128)(2,1)} %all-to-all-done.voltage_ref, bf16[8,2,2,512,1024]{4,3,2,1,0:T(8,128)(2,1)} %weight_ref.5), custom_call_target="tpu_custom_call" | custom-call | flops 8589934592 | bytes 37748736 | tf_op jit(solution)/shard_map/beams_0/pallas_call | solution.py:207
  269.6 17.5 %beams_1.1 = bf16[8,16,1024]{2,1,0:T(8,128)(2,1)S(1)} custom-call(bf16[32,16,32,128]{3,2,1,0:T(8,128)(2,1)} %all-to-all-done.1.voltage_ref, bf16[8,2,2,512,1024]{4,3,2,1,0:T(8,128)(2,1)} %weight_ref.5), custom_call_target="tpu_custom_call" | custom-call | flops 8589934592 | bytes 37748736 | tf_op jit(solution)/shard_map/beams_1/pallas_call | solution.py:207
  287.1 58.4 %all-to-all-done.2.voltage_ref = bf16[32,16,32,128]{3,2,1,0:T(8,128)(2,1)} async-done(((bf16[32,16,32,128]{3,2,1,0:T(8,128)(2,1)}), bf16[32,16,32,128]{3,2,1,0:T(8,128)(2,1)}, u32[]{:S(2)}, u32[]{:S(2)}) %all-to-all-start.2) | async-done | bytes 4194336 | tf_op jit(solution)/shard_map/all_to_all | solution.py:281
  345.5 17.5 %beams_2.1 = bf16[8,16,1024]{2,1,0:T(8,128)(2,1)S(1)} custom-call(bf16[32,16,32,128]{3,2,1,0:T(8,128)(2,1)} %all-to-all-done.2.voltage_ref, bf16[8,2,2,512,1024]{4,3,2,1,0:T(8,128)(2,1)} %weight_ref.5), custom_call_target="tpu_custom_call" | custom-call | flops 8589934592 | bytes 37748736 | tf_op jit(solution)/shard_map/beams_2/pallas_call | solution.py:207
  364.7 4.0 reshape.236
  368.8 3.5 all-to-all-start.3
  372.6 19.7 %all-to-all-done.3 = bf16[4,2,49152]{2,1,0:T(2,128)(2,1)S(1)} async-done(((bf16[4,2,49152]{2,1,0:T(2,128)(2,1)}), bf16[4,2,49152]{2,1,0:T(2,128)(2,1)S(1)}, u32[]{:S(2)}, u32[]{:S(2)}) %all-to-all-start.3) | async-done | bytes 786464 | tf_op jit(solution)/shard_map/all_to_all | solution.py:285
  392.3 2.1 reshape.237
  400.5 4.8 %collective-permute-start.1 = (bf16[16,48,256]{2,1,0:T(8,128)(2,1)}, bf16[16,48,256]{2,1,0:T(8,128)(2,1)}, u32[]{:S(2)}, u32[]{:S(2)}) collective-permute-start(bf16[16,48,256]{2,1,0:T(8,128)(2,1)} %bitcast.15), channel_id=1, source_target_pairs={{1,0},{2,1},{3,2},{4,3},{5,4},{6,5},{7,6},{9,8},{10,9},{11,10},{12... | collective-permute-start | bytes 1179656 | tf_op jit(solution)/shard_map/ppermute | solution.py:25
  405.2 3.3 convolution_bitcast_fusion
  408.5 3.6 copy.23
  412.1 5.7 %reshape.227 = f32[384,1920]{1,0:T(8,128)S(1)} reshape(f32[8,48,40,48]{3,2,1,0:T(8,128)} %copy.23) | data formatting | bytes 5898240 | tf_op jit(solution)/shard_map/reshape | solution.py:238
  (37 shorter events, 22.5 us)
Async XLA Ops:
  0.0 372.3 %copy-start = (f32[33,33]{1,0:T(8,128)S(1)}, f32[33,33]{1,0:T(8,128)}, u32[]{:S(2)}) copy-start(f32[33,33]{1,0:T(8,128)} %param.7) | copy-start | bytes 13072
  2.2 11.8 %copy-start.4 = (f32[16,256]{1,0:T(8,128)S(1)}, f32[16,256]{1,0:T(8,128)}, u32[]{:S(2)}) copy-start(f32[16,256]{1,0:T(8,128)} %taps_ref.5) | copy-start | bytes 49156
  48.1 2.0 copy-start.3
  50.1 99.6 %all-to-all-start = ((bf16[32,16,32,128]{3,2,1,0:T(8,128)(2,1)}), bf16[32,16,32,128]{3,2,1,0:T(8,128)(2,1)}, u32[]{:S(2)}, u32[]{:S(2)}) async-start(bf16[32,16,32,128]{3,2,1,0:T(8,128)(2,1)} %bitcast.53), calls=%async_computation | async-start | bytes 8388608 | tf_op jit(solution)/shard_map/all_to_all | solution.py:281
  90.4 2.0 copy-start.2
  149.6 97.9 %all-to-all-start.1 = ((bf16[32,16,32,128]{3,2,1,0:T(8,128)(2,1)}), bf16[32,16,32,128]{3,2,1,0:T(8,128)(2,1)}, u32[]{:S(2)}, u32[]{:S(2)}) async-start(bf16[32,16,32,128]{3,2,1,0:T(8,128)(2,1)} %bitcast.52), calls=%async_computation.1 | async-start | bytes 8388608 | tf_op jit(solution)/shard_map/all_to_all | solution.py:281
  188.3 2.0 copy-start.1
  247.6 97.9 %all-to-all-start.2 = ((bf16[32,16,32,128]{3,2,1,0:T(8,128)(2,1)}), bf16[32,16,32,128]{3,2,1,0:T(8,128)(2,1)}, u32[]{:S(2)}, u32[]{:S(2)}) async-start(bf16[32,16,32,128]{3,2,1,0:T(8,128)(2,1)} %bitcast.51), calls=%async_computation.2 | async-start | bytes 8388608 | tf_op jit(solution)/shard_map/all_to_all | solution.py:281
  368.8 23.6 %all-to-all-start.3 = ((bf16[4,2,49152]{2,1,0:T(2,128)(2,1)}), bf16[4,2,49152]{2,1,0:T(2,128)(2,1)S(1)}, u32[]{:S(2)}, u32[]{:S(2)}) async-start(bf16[4,2,49152]{2,1,0:T(2,128)(2,1)} %reshape.236), calls=%async_computation.3 | async-start | bytes 1572864 | tf_op jit(solution)/shard_map/all_to_all | solution.py:285
  396.2 12.3 %copy-start.5 = (bf16[8,48,4,256]{3,2,1,0:T(4,128)(2,1)}, bf16[8,48,4,256]{3,2,1,0:T(4,128)(2,1)S(1)}, u32[]{:S(2)}) copy-start(bf16[8,48,4,256]{3,2,1,0:T(4,128)(2,1)S(1)} %copy.32) | copy-start | bytes 2359300
  397.7 21.3 %collective-permute-start = (bf16[16,48,256]{2,1,0:T(8,128)(2,1)}, bf16[16,48,256]{2,1,0:T(8,128)(2,1)S(1)}, u32[]{:S(2)}, u32[]{:S(2)}) collective-permute-start(bf16[16,48,256]{2,1,0:T(8,128)(2,1)} %bitcast.13), channel_id=1, source_target_pairs={{0,1},{1,2},{2,3},{3,4},{4,5},{5,6},{6,7},{8,9},{9,10},{10,11},{11... | collective-permute-start | bytes 1179656 | tf_op jit(solution)/shard_map/ppermute | solution.py:22
  400.5 18.5 %collective-permute-start.1 = (bf16[16,48,256]{2,1,0:T(8,128)(2,1)}, bf16[16,48,256]{2,1,0:T(8,128)(2,1)}, u32[]{:S(2)}, u32[]{:S(2)}) collective-permute-start(bf16[16,48,256]{2,1,0:T(8,128)(2,1)} %bitcast.15), channel_id=1, source_target_pairs={{1,0},{2,1},{3,2},{4,3},{5,4},{6,5},{7,6},{9,8},{10,9},{11,10},{12... | collective-permute-start | bytes 1179656 | tf_op jit(solution)/shard_map/ppermute | solution.py:25

commit v2 on v1

--- a/solution.py
+++ b/solution.py
@@ -198,10 +198,13 @@
         power = squares[:spectra] + squares[spectra:]
         energy = power if energy is None else energy + power
     binned = energy.reshape(spectra // INTEG, INTEG, beams).sum(axis=1)
-    out_ref[0] = (binned * jnp.float32(1.0 / (pols * INTEG))).astype(jnp.bfloat16)
-
-
-def beam_power(turned, beam_weights, portion):
+    intensity = (binned * jnp.float32(1.0 / (pols * INTEG))).astype(jnp.bfloat16)
+    share = out_ref.shape[3]
+    for owner in range(out_ref.shape[0]):
+        out_ref[owner, 0] = intensity[:, owner * share : (owner + 1) * share]
+
+
+def beam_power(turned, beam_weights, portion, owners):
     sources, rows, inputs_each, spectra = turned.shape
     per_device, pols, _, dishes, beams = beam_weights.shape
     return pl.pallas_call(
@@ -211,8 +214,12 @@
             pl.BlockSpec((sources, 2, inputs_each, spectra), lambda c: (0, c, 0, 0)),
             pl.BlockSpec((1, pols, 2, dishes, beams), lambda c: (c, 0, 0, 0, 0)),
         ],
-        out_specs=pl.BlockSpec((1, spectra // INTEG, beams), lambda c: (c, 0, 0)),
-        out_shape=jax.ShapeDtypeStruct((per_device, spectra // INTEG, beams), jnp.bfloat16),
+        out_specs=pl.BlockSpec(
+            (owners, 1, spectra // INTEG, beams // owners), lambda c: (0, c, 0, 0)
+        ),
+        out_shape=jax.ShapeDtypeStruct(
+            (owners, per_device, spectra // INTEG, beams // owners), jnp.bfloat16
+        ),
         cost_estimate=pl.CostEstimate(
             flops=16 * per_device * dishes * spectra * beams,
             bytes_accessed=2 * beam_weights.size + 2 * turned.size,
@@ -280,9 +287,13 @@
         turned.append(
             lax.all_to_all(arranged, ("wide", "narrow"), split_axis=0, concat_axis=0, tiled=True)
         )
-    pieces = [beam_power(block, beam_weights, portion) for portion, block in enumerate(turned)]
-    intensity = jnp.concatenate(pieces, axis=1)
-    by_beam = lax.all_to_all(intensity, "wide", split_axis=2, concat_axis=0, tiled=True)
+    pieces = [
+        beam_power(block, beam_weights, portion, wide_count)
+        for portion, block in enumerate(turned)
+    ]
+    intensity = jnp.concatenate(pieces, axis=2)
+    by_beam = lax.all_to_all(intensity, "wide", split_axis=0, concat_axis=0, tiled=True)
+    by_beam = by_beam.reshape(-1, *by_beam.shape[2:])
     half_width = smooth_kernel.shape[0] // 2
     extended = with_halo(by_beam, (("narrow", 0),), half_width)
     return smooth(extended, matrix, half_width)

time: 431 us -> 420 us (0.974)
  local copies, waits for them, and re-layouts: 41.9 us -> 29.9 us
    unnamed x16, local copies, waits for them, and re-layouts: 23.9 us -> 17.8 us
  transfers between devices with their start and end apart: 6 -> 6, of which waited for: 4 -> 4; matrix products, arithmetic and copies ran while one was open for 3% -> 3% of each run, Pallas kernels for 24% -> 25%
where the time goes in v2:
time: 420 us; the launch traced here: 419 us
  waiting for transfers between devices  193 us (46%)
  Pallas kernels  155 us (37%)
  local copies, waits for them, and re-layouts  29.9 us (7%)
  starting transfers between devices  25.2 us (6%)
  matrix products  9.6 us (2%)
  other arithmetic  6.53 us (2%)
    all_to_all x3, waiting for transfers between devices, body(): lax.all_to_all(arranged, ('wide', 'narrow'), split_axis=0, concat_axis=0,...  173 us
    pallas_call x3, Pallas kernels, channelize(): pl.pallas_call(channelize_kernel, grid=(inputs_here // group,), in_specs=...  102 us
    pallas_call x3, Pallas kernels, beam_power(): pl.pallas_call(beam_kernel, grid=(per_device,), in_specs=[pl.BlockSpec((s...  52.4 us
    all_to_all x1, waiting for transfers between devices, body(): lax.all_to_all(intensity, 'wide', split_axis=0, concat_axis=0, tiled=True)  19.7 us
    unnamed x16, local copies, waits for them, and re-layouts  17.8 us
    all_to_all x3, starting transfers between devices, body(): lax.all_to_all(arranged, ('wide', 'narrow'), split_axis=0, concat_axis=0,...  15.2 us
  transfers between devices with their start and end apart: 6, of which 4 were waited for; matrix products, arithmetic and copies ran while one was open for 3% of the time, Pallas kernels for 25%

profile of v2, /device:TPU:4, one launch (start us, length us, event | category | flops | bytes accessed | tf_op | source)
XLA Modules:
  0.0 419.0 jit_solution(8642495716528268842)
XLA Ops:
  2.2 11.8 %copy.16 = bf16[32,2,102144]{2,0,1:T(8,128)(2,1)} copy(bf16[32,2,102144]{2,1,0:T(2,128)(2,1)} %param.4) | data formatting | bytes 26148864 | tf_op args[0]
  14.0 34.1 %channelize_0.1 = bf16[512,32,128]{2,1,0:T(8,128)(2,1)S(1)} custom-call(f32[16,256]{1,0:T(8,128)S(1)} %copy-done.4, f32[512,512]{1,0:T(8,128)S(1)} %bitcast.44, bf16[2,32,102144]{2,1,0:T(8,128)(2,1)} %bitcast.50, bf16[2,32,102144]{2,1,0:T(8,128)(2,1)} %bitcast.51), custom_call_target="tpu_custom_call" | custom-call | flops 6442450944 | bytes 8388608 | tf_op jit(solution)/shard_map/channelize_0/pallas_call | solution.py:148
  48.1 2.0 copy-done.3
  50.1 6.2 %all-to-all-start = ((bf16[32,16,32,128]{3,2,1,0:T(8,128)(2,1)}), bf16[32,16,32,128]{3,2,1,0:T(8,128)(2,1)}, u32[]{:S(2)}, u32[]{:S(2)}) async-start(bf16[32,16,32,128]{3,2,1,0:T(8,128)(2,1)} %bitcast.49), calls=%async_computation | async-start | bytes 8388608 | tf_op jit(solution)/shard_map/all_to_all | solution.py:288
  56.2 34.1 %channelize_1.1 = bf16[512,32,128]{2,1,0:T(8,128)(2,1)S(1)} custom-call(f32[16,256]{1,0:T(8,128)S(1)} %copy-done.4, f32[512,512]{1,0:T(8,128)S(1)} %bitcast.45, bf16[2,32,102144]{2,1,0:T(8,128)(2,1)} %bitcast.52, bf16[2,32,102144]{2,1,0:T(8,128)(2,1)} %bitcast.53), custom_call_target="tpu_custom_call" | custom-call | flops 6442450944 | bytes 8388608 | tf_op jit(solution)/shard_map/channelize_1/pallas_call | solution.py:148
  90.4 2.0 copy-done.2
  92.4 57.3 %all-to-all-done.voltage_ref = bf16[32,16,32,128]{3,2,1,0:T(8,128)(2,1)} async-done(((bf16[32,16,32,128]{3,2,1,0:T(8,128)(2,1)}), bf16[32,16,32,128]{3,2,1,0:T(8,128)(2,1)}, u32[]{:S(2)}, u32[]{:S(2)}) %all-to-all-start) | async-done | bytes 4194336 | tf_op jit(solution)/shard_map/all_to_all | solution.py:288
  149.6 4.5 %all-to-all-start.1 = ((bf16[32,16,32,128]{3,2,1,0:T(8,128)(2,1)}), bf16[32,16,32,128]{3,2,1,0:T(8,128)(2,1)}, u32[]{:S(2)}, u32[]{:S(2)}) async-start(bf16[32,16,32,128]{3,2,1,0:T(8,128)(2,1)} %bitcast.48), calls=%async_computation.1 | async-start | bytes 8388608 | tf_op jit(solution)/shard_map/all_to_all | solution.py:288
  154.2 34.1 %channelize_2.1 = bf16[512,32,128]{2,1,0:T(8,128)(2,1)S(1)} custom-call(f32[16,256]{1,0:T(8,128)S(1)} %copy-done.4, f32[512,512]{1,0:T(8,128)S(1)} %bitcast.46, bf16[2,32,102144]{2,1,0:T(8,128)(2,1)} %bitcast.54, bf16[2,32,102144]{2,1,0:T(8,128)(2,1)} %bitcast.55), custom_call_target="tpu_custom_call" | custom-call | flops 6442450944 | bytes 8388608 | tf_op jit(solution)/shard_map/channelize_2/pallas_call | solution.py:148
  188.3 1.9 copy-done.1
  190.3 57.3 %all-to-all-done.1.voltage_ref = bf16[32,16,32,128]{3,2,1,0:T(8,128)(2,1)} async-done(((bf16[32,16,32,128]{3,2,1,0:T(8,128)(2,1)}), bf16[32,16,32,128]{3,2,1,0:T(8,128)(2,1)}, u32[]{:S(2)}, u32[]{:S(2)}) %all-to-all-start.1) | async-done | bytes 4194336 | tf_op jit(solution)/shard_map/all_to_all | solution.py:288
  247.6 4.5 %all-to-all-start.2 = ((bf16[32,16,32,128]{3,2,1,0:T(8,128)(2,1)}), bf16[32,16,32,128]{3,2,1,0:T(8,128)(2,1)}, u32[]{:S(2)}, u32[]{:S(2)}) async-start(bf16[32,16,32,128]{3,2,1,0:T(8,128)(2,1)} %bitcast.47), calls=%async_computation.2 | async-start | bytes 8388608 | tf_op jit(solution)/shard_map/all_to_all | solution.py:288
  252.1 17.5 %beams_0.1 = bf16[4,8,16,256]{3,2,1,0:T(8,128)(2,1)S(1)} custom-call(bf16[32,16,32,128]{3,2,1,0:T(8,128)(2,1)} %all-to-all-done.voltage_ref, bf16[8,2,2,512,1024]{4,3,2,1,0:T(8,128)(2,1)} %weight_ref.5), custom_call_target="tpu_custom_call" | custom-call | flops 8589934592 | bytes 37748736 | tf_op jit(solution)/shard_map/beams_0/pallas_call | solution.py:210
  269.6 17.5 %beams_1.1 = bf16[4,8,16,256]{3,2,1,0:T(8,128)(2,1)S(1)} custom-call(bf16[32,16,32,128]{3,2,1,0:T(8,128)(2,1)} %all-to-all-done.1.voltage_ref, bf16[8,2,2,512,1024]{4,3,2,1,0:T(8,128)(2,1)} %weight_ref.5), custom_call_target="tpu_custom_call" | custom-call | flops 8589934592 | bytes 37748736 | tf_op jit(solution)/shard_map/beams_1/pallas_call | solution.py:210
  287.1 58.4 %all-to-all-done.2.voltage_ref = bf16[32,16,32,128]{3,2,1,0:T(8,128)(2,1)} async-done(((bf16[32,16,32,128]{3,2,1,0:T(8,128)(2,1)}), bf16[32,16,32,128]{3,2,1,0:T(8,128)(2,1)}, u32[]{:S(2)}, u32[]{:S(2)}) %all-to-all-start.2) | async-done | bytes 4194336 | tf_op jit(solution)/shard_map/all_to_all | solution.py:288
  345.5 17.5 %beams_2.1 = bf16[4,8,16,256]{3,2,1,0:T(8,128)(2,1)S(1)} custom-call(bf16[32,16,32,128]{3,2,1,0:T(8,128)(2,1)} %all-to-all-done.2.voltage_ref, bf16[8,2,2,512,1024]{4,3,2,1,0:T(8,128)(2,1)} %weight_ref.5), custom_call_target="tpu_custom_call" | custom-call | flops 8589934592 | bytes 37748736 | tf_op jit(solution)/shard_map/beams_2/pallas_call | solution.py:210
  363.9 3.5 all-to-all-start.3
  367.8 19.7 %all-to-all-done.3 = bf16[4,8,48,256]{3,2,1,0:T(8,128)(2,1)S(1)} async-done(((bf16[4,8,48,256]{3,2,1,0:T(8,128)(2,1)}), bf16[4,8,48,256]{3,2,1,0:T(8,128)(2,1)S(1)}, u32[]{:S(2)}, u32[]{:S(2)}) %all-to-all-start.3) | async-done | bytes 786464 | tf_op jit(solution)/shard_map/all_to_all | solution.py:295
  388.6 1.9 collective-permute-start
  390.5 4.5 %collective-permute-start.1 = (bf16[16,48,256]{2,1,0:T(8,128)(2,1)}, bf16[16,48,256]{2,1,0:T(8,128)(2,1)}, u32[]{:S(2)}, u32[]{:S(2)}) collective-permute-start(bf16[16,48,256]{2,1,0:T(8,128)(2,1)} %bitcast.13), channel_id=1, source_target_pairs={{1,0},{2,1},{3,2},{4,3},{5,4},{6,5},{7,6},{9,8},{10,9},{11,10},{12... | collective-permute-start | bytes 1179656 | tf_op jit(solution)/shard_map/ppermute | solution.py:25
  395.0 3.3 convolution_bitcast_fusion
  398.3 3.6 copy.10
  401.9 5.7 %reshape.230 = f32[384,1920]{1,0:T(8,128)S(1)} reshape(f32[8,48,40,48]{3,2,1,0:T(8,128)} %copy.10) | data formatting | bytes 5898240 | tf_op jit(solution)/shard_map/reshape | solution.py:245
  407.6 1.7 convert_reduce_fusion
  (32 shorter events, 14.1 us)
Async XLA Ops:
  0.0 367.5 %copy-start = (f32[33,33]{1,0:T(8,128)S(1)}, f32[33,33]{1,0:T(8,128)}, u32[]{:S(2)}) copy-start(f32[33,33]{1,0:T(8,128)} %param.7) | copy-start | bytes 13072
  2.2 11.8 %copy-start.4 = (f32[16,256]{1,0:T(8,128)S(1)}, f32[16,256]{1,0:T(8,128)}, u32[]{:S(2)}) copy-start(f32[16,256]{1,0:T(8,128)} %taps_ref.5) | copy-start | bytes 49156
  48.1 2.0 copy-start.3
  50.1 99.6 %all-to-all-start = ((bf16[32,16,32,128]{3,2,1,0:T(8,128)(2,1)}), bf16[32,16,32,128]{3,2,1,0:T(8,128)(2,1)}, u32[]{:S(2)}, u32[]{:S(2)}) async-start(bf16[32,16,32,128]{3,2,1,0:T(8,128)(2,1)} %bitcast.49), calls=%async_computation | async-start | bytes 8388608 | tf_op jit(solution)/shard_map/all_to_all | solution.py:288
  90.3 2.0 copy-start.2
  149.6 97.9 %all-to-all-start.1 = ((bf16[32,16,32,128]{3,2,1,0:T(8,128)(2,1)}), bf16[32,16,32,128]{3,2,1,0:T(8,128)(2,1)}, u32[]{:S(2)}, u32[]{:S(2)}) async-start(bf16[32,16,32,128]{3,2,1,0:T(8,128)(2,1)} %bitcast.48), calls=%async_computation.1 | async-start | bytes 8388608 | tf_op jit(solution)/shard_map/all_to_all | solution.py:288
  188.3 2.0 copy-start.1
  247.6 97.9 %all-to-all-start.2 = ((bf16[32,16,32,128]{3,2,1,0:T(8,128)(2,1)}), bf16[32,16,32,128]{3,2,1,0:T(8,128)(2,1)}, u32[]{:S(2)}, u32[]{:S(2)}) async-start(bf16[32,16,32,128]{3,2,1,0:T(8,128)(2,1)} %bitcast.47), calls=%async_computation.2 | async-start | bytes 8388608 | tf_op jit(solution)/shard_map/all_to_all | solution.py:288
  363.9 23.6 %all-to-all-start.3 = ((bf16[4,8,48,256]{3,2,1,0:T(8,128)(2,1)}), bf16[4,8,48,256]{3,2,1,0:T(8,128)(2,1)S(1)}, u32[]{:S(2)}, u32[]{:S(2)}) async-start(bf16[4,8,48,256]{3,2,1,0:T(8,128)(2,1)} %pad_maximum_fusion.3), calls=%async_computation.3 | async-start | bytes 1572864 | tf_op jit(solution)/shard_map/all_to_all | solution.py:295
  387.5 10.8 %copy-start.5 = (bf16[4,8,48,256]{3,2,1,0:T(8,128)(2,1)}, bf16[4,8,48,256]{3,2,1,0:T(8,128)(2,1)S(1)}, u32[]{:S(2)}) copy-start(bf16[4,8,48,256]{3,2,1,0:T(8,128)(2,1)S(1)} %all-to-all-done.3) | copy-start | bytes 2359300
  388.6 19.0 %collective-permute-start = (bf16[16,48,256]{2,1,0:T(8,128)(2,1)}, bf16[16,48,256]{2,1,0:T(8,128)(2,1)S(1)}, u32[]{:S(2)}, u32[]{:S(2)}) collective-permute-start(bf16[16,48,256]{2,1,0:T(8,128)(2,1)} %bitcast.11), channel_id=1, source_target_pairs={{0,1},{1,2},{2,3},{3,4},{4,5},{5,6},{6,7},{8,9},{9,10},{10,11},{11... | collective-permute-start | bytes 1179656 | tf_op jit(solution)/shard_map/ppermute | solution.py:22
  390.5 17.1 %collective-permute-start.1 = (bf16[16,48,256]{2,1,0:T(8,128)(2,1)}, bf16[16,48,256]{2,1,0:T(8,128)(2,1)}, u32[]{:S(2)}, u32[]{:S(2)}) collective-permute-start(bf16[16,48,256]{2,1,0:T(8,128)(2,1)} %bitcast.13), channel_id=1, source_target_pairs={{1,0},{2,1},{3,2},{4,3},{5,4},{6,5},{7,6},{9,8},{10,9},{11,10},{12... | collective-permute-start | bytes 1179656 | tf_op jit(solution)/shard_map/ppermute | solution.py:25
  407.5 1.8 copy-start.6
